TPU v7x, 512 devices: a whole 4x4x16 slice. The times are simulated.
512 devices in a mesh: term: 8 (over y, core), doc: 16 (over z), enc: 4 (over x).
Axes of the slice: x: 4, y: 4, z: 16, core: 2. Of those that a mesh axis runs over, the one named last changes fastest.
Arguments:
- query_weights: bfloat16 [1024, 30720], P('enc', ('term', 'doc')), may hold values from 0.049804688 to 2
- tile_terms: int32 [30720], P(('term', 'doc')), may hold values from 0 to 59
- tile_blocks: int32 [30720], P(('term', 'doc')), may hold values from 0 to 15
- tile_counts: int32 [128], P(('term', 'doc')), may hold values from 60 to 240, as said below
- impacts: bfloat16 [30720, 64, 128], P(('term', 'doc')), may hold values from -0.015625 to 0.015625
Outputs:
- scores: float32 [2048, 1024], P('doc', 'enc')
Inputs may be any that keep to these rules, and one draw needn't show every extreme that they name: Slots at positions tile_counts or later of a device's list are padding and contribute nothing; some device has all 240 slots live.
All inputs are finite; a program needn't handle non-finite values.
Results may differ from a plain program's by a relative error of at most 0.0003.
Values may be sent and summed in bfloat16 or wider, within the bound.
No kernel may reach another device: no remote copies, remote signals or barrier semaphores. Data moves between devices by JAX's collectives and lax.ppermute only.
A program may use at most 64 MiB of HBM per device.

v0:
```python
import jax
import jax.numpy as jnp
from jax import lax
from jax.sharding import PartitionSpec as P


def block_size(tiles):
    largest = 1
    for divisor in range(1, 65):
        if tiles % divisor == 0:
            largest = divisor
    return largest


def per_device(query_weights, tile_terms, tile_blocks, tile_counts, impacts):
    range_rows = lax.all_gather(query_weights, "doc", axis=1, tiled=True)
    queries = range_rows.shape[0]
    tiles, term_block, doc_block = impacts.shape
    owners = lax.axis_size("doc")
    grouped = range_rows.reshape(queries, range_rows.shape[1] // term_block, term_block)
    step = block_size(tiles)
    live = jnp.arange(tiles, dtype=jnp.int32) < tile_counts[0]
    owner_ids = jnp.arange(owners, dtype=jnp.int32)

    def accumulate(total, number):
        start = number * step
        term_now = lax.dynamic_slice_in_dim(tile_terms, start, step)
        owner_now = lax.dynamic_slice_in_dim(tile_blocks, start, step)
        keep_now = lax.dynamic_slice_in_dim(live, start, step)
        tile_now = lax.dynamic_slice_in_dim(impacts, start, step)
        picked = jnp.take(grouped, term_now, axis=1)
        product = jnp.einsum("qnk,nkd->ndq", picked, tile_now, preferred_element_type=jnp.float32)
        select = ((owner_now[:, None] == owner_ids[None, :]) & keep_now[:, None]).astype(
            jnp.float32
        )
        added = jnp.einsum("ndq,nb->bdq", product, select, precision=lax.Precision.HIGHEST)
        return (total + added, None)

    start_total = jnp.zeros((owners, doc_block, queries), jnp.float32)
    total, unused = lax.scan(accumulate, start_total, jnp.arange(tiles // step, dtype=jnp.int32))
    partial_value = total.reshape(owners * doc_block, queries)
    mine = lax.psum_scatter(partial_value, "doc", scatter_dimension=0, tiled=True)
    scores = lax.psum(mine, "term")
    return scores


def solution(mesh):
    return jax.shard_map(
        per_device,
        mesh=mesh,
        in_specs=(
            P("enc", ("term", "doc")),
            P(("term", "doc")),
            P(("term", "doc")),
            P(("term", "doc")),
            P(("term", "doc"), None, None),
        ),
        out_specs=P("doc", "enc"),
        check_vma=False,
    )
```

profile of v0, /device:TPU:2, one launch (start us, length us, event | category | flops | bytes accessed | tf_op | source)
XLA Modules:
  0.0 312.8 jit_solution(1491762189442942286)
XLA Ops:
  8.0 78.3 %all-gather.2.cloned.1.call-done = bf16[256,3840]{0,1:T(8,128)(2,1)} async-done(((bf16[256,240]{0,1:T(8,128)(2,1)}), bf16[256,3840]{0,1:T(8,128)(2,1)}) %all-gather.2.cloned.1.call-update) | async-done | bytes 1966096 | tf_op jit(solution)/shard_map/all_gather | solution.py:16
  86.2 67.8 %while.11 = (s32[]{:T(128)}, f32[16,128,256]{2,0,1:T(8,128)}, s32[4]{0:T(128)S(1)}, s32[240]{0:T(256)}, pred[240]{0:T(512)(128)(4,1)S(1)}, /*index=5*/bf16[240,6...) while((s32[]{:T(128)}, f32[16,128,256]{2,0,1:T(8,128)}, ...), condition=%wide.region_1.2_spmd.clone, body=%wide.region_0.1_spmd.clone.sunk | while | flops 631180544 | bytes 43587780 | solution.py:40
  88.3 0.8 compare_and_fusion.2
  89.1 2.2 gather_fusion
  91.3 2.6 fusion.28
  93.9 7.9 %select_add_fusion.2 = f32[16,128,256]{2,0,1:T(8,128)S(1)} fusion(f32[16,128,256]{2,0,1:T(8,128)S(1)} %copy-done, f32[60,128,256]{2,1,0:T(8,128)S(1)} %fusion.28, pred[]{:T(512)S(6)} %compare.3, s32[60]{0:T(128)S(1)} %dynamic_slice.31, pred[60]{0:T(512)(128)(4,1)S(1)} %dynamic_slice.32), kind=kOutput, calls=%fused_computation.4.clone.1 | convolution fusion | flops 378537856 | bytes 12058925 | tf_op jit(solution)/shard_map/while/body/eval_jaxpr/ndq,nb->bdq/dot_general | solution.py:36
  101.9 1.3 copy-done.1
  105.2 0.8 compare_and_fusion.2
  106.0 2.2 gather_fusion
  108.3 2.6 fusion.28
  110.9 7.9 %select_add_fusion.2 = f32[16,128,256]{2,0,1:T(8,128)S(1)} fusion(f32[16,128,256]{2,0,1:T(8,128)S(1)} %copy-done, f32[60,128,256]{2,1,0:T(8,128)S(1)} %fusion.28, pred[]{:T(512)S(6)} %compare.3, s32[60]{0:T(128)S(1)} %dynamic_slice.31, pred[60]{0:T(512)(128)(4,1)S(1)} %dynamic_slice.32), kind=kOutput, calls=%fused_computation.4.clone.1 | convolution fusion | flops 378537856 | bytes 12058925 | tf_op jit(solution)/shard_map/while/body/eval_jaxpr/ndq,nb->bdq/dot_general | solution.py:36
  118.8 1.3 copy-done.1
  122.9 2.2 gather_fusion
  125.2 2.6 fusion.28
  127.8 7.9 %select_add_fusion.2 = f32[16,128,256]{2,0,1:T(8,128)S(1)} fusion(f32[16,128,256]{2,0,1:T(8,128)S(1)} %copy-done, f32[60,128,256]{2,1,0:T(8,128)S(1)} %fusion.28, pred[]{:T(512)S(6)} %compare.3, s32[60]{0:T(128)S(1)} %dynamic_slice.31, pred[60]{0:T(512)(128)(4,1)S(1)} %dynamic_slice.32), kind=kOutput, calls=%fused_computation.4.clone.1 | convolution fusion | flops 378537856 | bytes 12058925 | tf_op jit(solution)/shard_map/while/body/eval_jaxpr/ndq,nb->bdq/dot_general | solution.py:36
  135.7 1.3 copy-done.1
  139.9 2.2 gather_fusion
  142.1 2.6 fusion.28
  144.8 7.9 %select_add_fusion.2 = f32[16,128,256]{2,0,1:T(8,128)S(1)} fusion(f32[16,128,256]{2,0,1:T(8,128)S(1)} %copy-done, f32[60,128,256]{2,1,0:T(8,128)S(1)} %fusion.28, pred[]{:T(512)S(6)} %compare.3, s32[60]{0:T(128)S(1)} %dynamic_slice.31, pred[60]{0:T(512)(128)(4,1)S(1)} %dynamic_slice.32), kind=kOutput, calls=%fused_computation.4.clone.1 | convolution fusion | flops 378537856 | bytes 12058925 | tf_op jit(solution)/shard_map/while/body/eval_jaxpr/ndq,nb->bdq/dot_general | solution.py:36
  152.7 1.3 copy-done.1
  154.0 4.1 %copy.8 = f32[16,128,256]{2,1,0:T(8,128)} copy(f32[16,128,256]{2,0,1:T(8,128)} %get-tuple-element.52) | data formatting | bytes 4194304 | tf_op jit(solution)/shard_map/while | solution.py:40
  158.2 71.0 %reduce-scatter.2.cloned.1.call-done = f32[128,256]{1,0:T(8,128)} async-done(((f32[2048,256]{1,0:T(8,128)}), f32[128,256]{1,0:T(8,128)}) %reduce-scatter.2.cloned.1.call-update) | async-done | bytes 131088 | tf_op jit(solution)/shard_map/reduce_scatter | solution.py:42
  229.3 75.4 %all-reduce.2.cloned.1.call-done = f32[128,256]{1,0:T(8,128)} async-done(((f32[128,256]{1,0:T(8,128)}), f32[128,256]{1,0:T(8,128)}) %all-reduce.2.cloned.1.call-update) | async-done | bytes 131088 | tf_op jit(solution)/shard_map/psum | solution.py:43
  304.7 1.6 copy.24
  (39 shorter events, 8.1 us)
Async XLA Ops:
  6.5 79.7 %all-gather.2.cloned.1.call-start = ((), (), s32[]{:S(2)}) async-start(), calls=%async_computation.1 | async-start | bytes 2088960 | tf_op jit(solution)/shard_map/all_gather | solution.py:16
  7.3 222.0 %reduce-scatter.2.cloned.1.call-start = ((), (), s32[]{:S(2)}) async-start(), calls=%async_computation.2 | async-start | bytes 2228224 | tf_op jit(solution)/shard_map/reduce_scatter | solution.py:42
  91.3 2.6 copy-start
  101.8 1.3 copy-start.1
  108.2 2.6 copy-start
  118.8 1.3 copy-start.1
  125.2 2.6 copy-start
  135.7 1.3 copy-start.1
  142.1 2.6 copy-start
  152.7 1.3 copy-start.1
  158.2 146.6 %all-reduce.2.cloned.1.call-start = ((), (), s32[]{:S(2)}) async-start(), calls=%async_computation.3 | async-start | bytes 262144 | tf_op jit(solution)/shard_map/psum | solution.py:43
Sparse Core Ops, SparseCore 0:
  9.4 76.7 all-gather.1
  158.3 70.9 reduce-scatter.1
  231.6 73.0 all-reduce.1
where the time goes:
time: 313 us
  waiting for transfers between devices  225 us (72%)
  matrix products  42 us (13%)
  local copies, waits for them, and re-layouts  25.7 us (8%)
  between operations  13.8 us (4%)
    all_gather x1, waiting for transfers between devices, per_device(): range_rows = lax.all_gather(query_weights, 'doc', axis=1, tiled=True)  78.3 us
    psum x1, waiting for transfers between devices, per_device(): scores = lax.psum(mine, 'term')  75.4 us
    reduce_scatter x1, waiting for transfers between devices, per_device(): lax.psum_scatter(partial_value, 'doc', scatter_dimension=0, tiled=True)  71 us
    dot_general x4, matrix products, accumulate(): jnp.einsum('ndq,nb->bdq', product, select, precision=lax.Precision.HIGHEST)  31.6 us
    dot_general x4, matrix products, accumulate(): jnp.einsum('qnk,nkd->ndq', picked, tile_now, preferred_element_type=jnp.f...  10.5 us
    gather x4, local copies, waits for them, and re-layouts, accumulate(): picked = jnp.take(grouped, term_now, axis=1)  8.92 us
  transfers between devices with their start and end apart: 3, of which 3 were waited for; matrix products, arithmetic and copies ran while one was open for 0% of the time, Pallas kernels for 0%

commit v1 on v0

--- a/solution.py
+++ b/solution.py
@@ -2,6 +2,11 @@
 import jax.numpy as jnp
 from jax import lax
 from jax.sharding import PartitionSpec as P
+
+
+def domain_spread(view):
+    arr_out = jax.lax.all_gather(view, axis_name="term")
+    return jnp.sum(arr_out, axis=0)
 
 
 def block_size(tiles):
@@ -40,7 +45,7 @@
     total, unused = lax.scan(accumulate, start_total, jnp.arange(tiles // step, dtype=jnp.int32))
     partial_value = total.reshape(owners * doc_block, queries)
     mine = lax.psum_scatter(partial_value, "doc", scatter_dimension=0, tiled=True)
-    scores = lax.psum(mine, "term")
+    scores = domain_spread(mine)
     return scores
 
 

time: 313 us -> 270 us (0.86)
  the two profiles are of different devices: /device:TPU:2 before, /device:TPU:1 now
where the time goes in v1:
time: 270 us
  waiting for transfers between devices  182 us (67%)
  matrix products  42 us (16%)
  local copies, waits for them, and re-layouts  24.1 us (9%)
  between operations  13.8 us (5%)
  other arithmetic  5.01 us (2%)
  loops' own time  2.71 us (1%)
    reduce_scatter x1, waiting for transfers between devices, per_device(): lax.psum_scatter(partial_value, 'doc', scatter_dimension=0, tiled=True)  69.9 us
    all_gather x1, waiting for transfers between devices, per_device(): range_rows = lax.all_gather(query_weights, 'doc', axis=1, tiled=True)  69.7 us
    all_gather x1, waiting for transfers between devices, domain_spread(): arr_out = jax.lax.all_gather(view, axis_name='term')  41.8 us
    dot_general x4, matrix products, accumulate(): jnp.einsum('ndq,nb->bdq', product, select, precision=lax.Precision.HIGHEST)  31.6 us
    dot_general x4, matrix products, accumulate(): jnp.einsum('qnk,nkd->ndq', picked, tile_now, preferred_element_type=jnp.f...  10.5 us
    gather x4, local copies, waits for them, and re-layouts, accumulate(): picked = jnp.take(grouped, term_now, axis=1)  8.92 us
  transfers between devices with their start and end apart: 3, of which 3 were waited for; matrix products, arithmetic and copies ran while one was open for 0% of the time, Pallas kernels for 0%

profile of v1, /device:TPU:1, one launch (start us, length us, event | category | flops | bytes accessed | tf_op | source)
XLA Modules:
  0.0 269.9 jit_solution(14714945664040734543)
XLA Ops:
  8.0 69.7 %all-gather.4.cloned.1.call-done = bf16[256,3840]{0,1:T(8,128)(2,1)} async-done(((bf16[256,240]{0,1:T(8,128)(2,1)}), bf16[256,3840]{0,1:T(8,128)(2,1)}) %all-gather.4.cloned.1.call-update) | async-done | bytes 1966096 | tf_op jit(solution)/shard_map/all_gather | solution.py:21
  77.7 67.8 %while.11 = (s32[]{:T(128)}, f32[16,128,256]{2,0,1:T(8,128)}, s32[4]{0:T(128)S(1)}, s32[240]{0:T(256)}, pred[240]{0:T(512)(128)(4,1)S(1)}, /*index=5*/bf16[240,6...) while((s32[]{:T(128)}, f32[16,128,256]{2,0,1:T(8,128)}, ...), condition=%wide.region_1.2_spmd.clone, body=%wide.region_0.1_spmd.clone.sunk | while | flops 631180544 | bytes 43587780 | solution.py:45
  79.7 0.8 compare_and_fusion.2
  80.5 2.2 gather_fusion
  82.8 2.6 fusion.28
  85.4 7.9 %select_add_fusion.2 = f32[16,128,256]{2,0,1:T(8,128)S(1)} fusion(f32[16,128,256]{2,0,1:T(8,128)S(1)} %copy-done, f32[60,128,256]{2,1,0:T(8,128)S(1)} %fusion.28, pred[]{:T(512)S(6)} %compare.3, s32[60]{0:T(128)S(1)} %dynamic_slice.31, pred[60]{0:T(512)(128)(4,1)S(1)} %dynamic_slice.32), kind=kOutput, calls=%fused_computation.4.clone.1 | convolution fusion | flops 378537856 | bytes 12058925 | tf_op jit(solution)/shard_map/while/body/eval_jaxpr/ndq,nb->bdq/dot_general | solution.py:41
  93.3 1.3 copy-done.1
  96.7 0.8 compare_and_fusion.2
  97.5 2.2 gather_fusion
  99.7 2.6 fusion.28
  102.3 7.9 %select_add_fusion.2 = f32[16,128,256]{2,0,1:T(8,128)S(1)} fusion(f32[16,128,256]{2,0,1:T(8,128)S(1)} %copy-done, f32[60,128,256]{2,1,0:T(8,128)S(1)} %fusion.28, pred[]{:T(512)S(6)} %compare.3, s32[60]{0:T(128)S(1)} %dynamic_slice.31, pred[60]{0:T(512)(128)(4,1)S(1)} %dynamic_slice.32), kind=kOutput, calls=%fused_computation.4.clone.1 | convolution fusion | flops 378537856 | bytes 12058925 | tf_op jit(solution)/shard_map/while/body/eval_jaxpr/ndq,nb->bdq/dot_general | solution.py:41
  110.2 1.3 copy-done.1
  114.4 2.2 gather_fusion
  116.6 2.6 fusion.28
  119.3 7.9 %select_add_fusion.2 = f32[16,128,256]{2,0,1:T(8,128)S(1)} fusion(f32[16,128,256]{2,0,1:T(8,128)S(1)} %copy-done, f32[60,128,256]{2,1,0:T(8,128)S(1)} %fusion.28, pred[]{:T(512)S(6)} %compare.3, s32[60]{0:T(128)S(1)} %dynamic_slice.31, pred[60]{0:T(512)(128)(4,1)S(1)} %dynamic_slice.32), kind=kOutput, calls=%fused_computation.4.clone.1 | convolution fusion | flops 378537856 | bytes 12058925 | tf_op jit(solution)/shard_map/while/body/eval_jaxpr/ndq,nb->bdq/dot_general | solution.py:41
  127.2 1.3 copy-done.1
  131.3 2.2 gather_fusion
  133.6 2.6 fusion.28
  136.2 7.9 %select_add_fusion.2 = f32[16,128,256]{2,0,1:T(8,128)S(1)} fusion(f32[16,128,256]{2,0,1:T(8,128)S(1)} %copy-done, f32[60,128,256]{2,1,0:T(8,128)S(1)} %fusion.28, pred[]{:T(512)S(6)} %compare.3, s32[60]{0:T(128)S(1)} %dynamic_slice.31, pred[60]{0:T(512)(128)(4,1)S(1)} %dynamic_slice.32), kind=kOutput, calls=%fused_computation.4.clone.1 | convolution fusion | flops 378537856 | bytes 12058925 | tf_op jit(solution)/shard_map/while/body/eval_jaxpr/ndq,nb->bdq/dot_general | solution.py:41
  144.1 1.3 copy-done.1
  145.5 4.1 %copy.7 = f32[16,128,256]{2,1,0:T(8,128)} copy(f32[16,128,256]{2,0,1:T(8,128)} %get-tuple-element.52) | data formatting | bytes 4194304 | tf_op jit(solution)/shard_map/while | solution.py:45
  149.6 69.9 %reduce-scatter.2.cloned.1.call-done = f32[128,256]{1,0:T(8,128)} async-done(((f32[2048,256]{1,0:T(8,128)}), f32[128,256]{1,0:T(8,128)}) %reduce-scatter.2.cloned.1.call-update) | async-done | bytes 131088 | tf_op jit(solution)/shard_map/reduce_scatter | solution.py:47
  219.6 41.8 %all-gather.6.cloned.1.call-done = f32[1024,256]{1,0:T(8,128)} async-done(((f32[128,256]{1,0:T(8,128)}), f32[1024,256]{1,0:T(8,128)}) %all-gather.6.cloned.1.call-update) | async-done | bytes 1048592 | tf_op jit(solution)/shard_map/all_gather | solution.py:8
  261.4 2.0 reduce_sum.9
  (39 shorter events, 8.1 us)
Async XLA Ops:
  6.5 71.2 %all-gather.4.cloned.1.call-start = ((), (), s32[]{:S(2)}) async-start(), calls=%async_computation.1 | async-start | bytes 2088960 | tf_op jit(solution)/shard_map/all_gather | solution.py:21
  7.3 212.3 %reduce-scatter.2.cloned.1.call-start = ((), (), s32[]{:S(2)}) async-start(), calls=%async_computation.2 | async-start | bytes 2228224 | tf_op jit(solution)/shard_map/reduce_scatter | solution.py:47
  82.7 2.6 copy-start
  93.3 1.3 copy-start.1
  99.7 2.6 copy-start
  110.2 1.3 copy-start.1
  116.6 2.6 copy-start
  127.2 1.3 copy-start.1
  133.6 2.6 copy-start
  144.1 1.3 copy-start.1
  149.6 111.8 %all-gather.6.cloned.1.call-start = ((), (), s32[]{:S(2)}) async-start(), calls=%async_computation.3 | async-start | bytes 1179648 | tf_op jit(solution)/shard_map/all_gather | solution.py:8
Sparse Core Ops, SparseCore 0:
  9.4 68.2 all-gather.3
  149.7 69.8 reduce-scatter.1
  221.7 39.6 all-gather.5
